TPU v7x, 128 devices: a whole 4x4x4 slice. The times are simulated.
128 devices in a mesh: mem: 8 (over x, core), tile: 16 (over z, y).
Axes of the slice: x: 4, y: 4, z: 4, core: 2. Of those that a mesh axis runs over, the one named last changes fastest.
Arguments:
- members: bfloat16 [16, 137, 8192], P('mem', None, 'tile'), may hold values from -18 to 18
- vertical: bfloat16 [137, 137], replicated, may hold values from 0 to 1, as said below
- jacobian: bfloat16 [2048, 231, 137], P('tile'), may hold values from -0.5 to 0.5
- sketch_bits: int32 [3, 2048, 231], P(None, 'tile'), may hold values from 0 to 1
- test_bits: int32 [3, 2048, 231], P(None, 'tile'), may hold values from 0 to 1
- obs_column: int32 [2048], P('tile'), may hold values from 0 to 8191, as said below
- obs_slot: int32 [2048], P('tile'), may hold values from 0 to 31, as said below
Outputs:
- image_q: float32 [3, 2048, 231], P(None, 'tile')
- image_w: float32 [3, 2048, 231], P(None, 'tile')
- trace_mean: float32 [], replicated
- sketch_rayleigh: float32 [], replicated
Inputs may be any that keep to these rules, and one draw needn't show every extreme that they name: The observations of owner d are rows d * 128 to (d + 1) * 128 - 1; an observation's column lies in tile obs_column // 512. `obs_slot`: among one owner's observations whose columns lie in the same tile the slots are distinct, so at most 32 of them lie in one tile; every owner has exactly 32 observations in some tile. A vertical correlation matrix: symmetric, positive semidefinite, with ones on the diagonal.
All inputs are finite; a program needn't handle non-finite values.
Results may differ from a plain program's by a relative error of at most 0.0053.
Values may be sent and summed in bfloat16 or wider, within the bound.
No kernel may reach another device: no remote copies, remote signals or barrier semaphores. Data moves between devices by JAX's collectives and lax.ppermute only.
A program may use at most 128 MiB of HBM per device.

v0:
```python
import jax
import jax.numpy as jnp
from jax import lax
from jax.sharding import Mesh
from jax.sharding import PartitionSpec as P

CB = 32
K = 3
STEPS = 6
TILE = ("tile_0", "tile_1")
diffusion_rate = 0.2
highest = lax.Precision.HIGHEST


def with_halo(block, sides, width):
    for axis, dim in sides:
        count = lax.axis_size(axis)
        forward = [(i, i + 1) for i in range(count - 1)]
        forward.append((count - 1, 0))
        backward = [(target, source) for source, target in forward]
        low = lax.ppermute(
            lax.slice_in_dim(block, block.shape[dim] - width, None, axis=dim), axis, forward
        )
        high = lax.ppermute(lax.slice_in_dim(block, 0, width, axis=dim), axis, backward)
        block = jnp.concatenate([low, block, high], axis=dim)
    return block


def gather_turned(arrays, axis, dims):
    turned = [jnp.moveaxis(a, dim, 0) for a, dim in zip(arrays, dims)]
    widths = [t[0].size for t in turned]
    both = jnp.concatenate([t.reshape(-1, w) for t, w in zip(turned, widths)], axis=1)
    whole = lax.all_gather(both, axis, axis=0, tiled=True)
    pieces = jnp.split(whole, [sum(widths[:k]) for k in range(1, len(widths))], axis=1)
    return tuple(
        (
            jnp.moveaxis(b.reshape(-1, *t.shape[1:]), 0, dim)
            for b, t, dim in zip(pieces, turned, dims)
        )
    )


def split_up(value, dim, peers):
    before, after = (value.shape[:dim], value.shape[dim + 1 :])
    return jnp.moveaxis(value.reshape(*before, peers, -1, *after), dim, 0)


def sum_at_owner(value, axis, dim):
    pieces = split_up(value, dim, lax.axis_size(axis))
    arrived = lax.all_to_all(pieces, axis, split_axis=0, concat_axis=0, tiled=True)
    return arrived.sum(axis=0)


def from_everyone(value, axis):
    peers = lax.axis_size(axis)
    return lax.all_to_all(
        jnp.broadcast_to(value[None], (peers, *value.shape)), axis, 0, 0, tiled=True
    )


def joined_along(pieces, dim):
    lengths = list(pieces.shape[1:])
    lengths[dim] *= pieces.shape[0]
    return jnp.moveaxis(pieces, 0, dim).reshape(lengths)


def collect_2(value, axis, dim):
    pieces = from_everyone(value, axis)
    return joined_along(pieces, dim)


def by_axis(value, axes):
    for axis in axes:
        value = lax.psum(value, axis)
    return value


def relax(extended):
    length = extended.shape[-1] - 2 * CB
    center = extended[..., CB : CB + length]
    places = jnp.arange(length) % CB
    west_ok = (places > 0).astype(jnp.float32)
    east_ok = (places < CB - 1).astype(jnp.float32)
    north = extended[..., :length]
    south = extended[..., 2 * CB :]
    west = extended[..., CB - 1 : CB - 1 + length]
    east = extended[..., CB + 1 : CB + 1 + length]
    return center + diffusion_rate * (
        north - center + (south - center) + west_ok * (west - center) + east_ok * (east - center)
    )


def diffuse(state):
    extended = with_halo(state, ((TILE, 2),), STEPS * CB)
    for _ in range(STEPS):
        extended = relax(extended)
    return extended


def on_device(members, vertical, jacobian, sketch_bits, test_bits, obs_column, obs_slot):
    tile_count = lax.axis_size(TILE)
    my_tile = lax.axis_index(TILE)
    obs_local = obs_column.shape[0]
    levels = members.shape[1]
    cell_count = members.shape[2]
    channels = jacobian.shape[1]
    capacity = obs_local // 4
    slot_count = tile_count * capacity
    ensemble = members.shape[0] * lax.axis_size("mem")
    count = float(obs_local * tile_count * channels)
    all_columns, all_slots = gather_turned((obs_column, obs_slot), TILE, (0, 0))
    owners = jnp.arange(tile_count * obs_local, dtype=jnp.int32) // obs_local
    target = jnp.where(
        all_columns // cell_count == my_tile, owners * capacity + all_slots, slot_count
    )
    cell_table = (
        jnp.zeros((slot_count,), jnp.int32).at[target].set(all_columns % cell_count, mode="drop")
    )
    occupied = jnp.zeros((slot_count,), jnp.bool_).at[target].set(True, mode="drop")
    spread = ((cell_table[:, None] == jnp.arange(cell_count)[None, :]) & occupied[:, None]).astype(
        jnp.bfloat16
    )
    my_positions = obs_column // cell_count * capacity + obs_slot
    collect = (my_positions[:, None] == jnp.arange(slot_count)[None, :]).astype(jnp.bfloat16)

    def apply_operator(vectors):
        probes = vectors.shape[0]
        rows = probes * levels
        adjoint = jnp.einsum(
            "ocl,poc->plo",
            jacobian,
            vectors.astype(jnp.bfloat16),
            preferred_element_type=jnp.float32,
        ).astype(jnp.bfloat16)
        outgoing = jnp.dot(
            adjoint.reshape(rows, obs_local), collect, preferred_element_type=jnp.float32
        ).astype(jnp.bfloat16)
        arrived = lax.all_to_all(outgoing, TILE, split_axis=1, concat_axis=1, tiled=True)
        field_sum = jnp.dot(arrived, spread, preferred_element_type=jnp.float32).reshape(
            probes, levels, cell_count
        )

        def member_step(number, carry):
            member = lax.dynamic_index_in_dim(members, number, 0, keepdims=False).astype(
                jnp.float32
            )
            product = (member[None] * field_sum).astype(jnp.bfloat16)
            mixed = jnp.einsum("kl,plc->pkc", vertical, product, preferred_element_type=jnp.float32)
            return carry + member[None] * diffuse(mixed)

        partial_sum = lax.fori_loop(
            0, members.shape[0], member_step, jnp.zeros((probes, levels, cell_count), jnp.float32)
        )
        partial_cols = jnp.take(partial_sum.reshape(rows, cell_count), cell_table, axis=1).reshape(
            rows, tile_count, capacity
        )
        picked = sum_at_owner(partial_cols, "mem", 2) / (ensemble - 1)
        outbound = picked.astype(jnp.bfloat16)
        returned = lax.all_to_all(outbound, TILE, split_axis=1, concat_axis=1, tiled=True)
        returned = collect_2(returned, "mem", 2)
        returned = returned.reshape(rows, slot_count)
        profile = jnp.dot(returned, collect.T, preferred_element_type=jnp.float32).astype(
            jnp.bfloat16
        )
        profile = profile.reshape(probes, levels, obs_local)
        return jnp.einsum("ocl,plo->poc", jacobian, profile, preferred_element_type=jnp.float32)

    sketch = (2 * sketch_bits - 1).astype(jnp.float32)
    test = (2 * test_bits - 1).astype(jnp.float32)
    sketch_image = apply_operator(sketch)
    products = by_axis(
        jnp.einsum("ioc,joc->ij", sketch_image, sketch_image, precision=highest), TILE
    )
    lower = jnp.linalg.cholesky(products)
    inverse_lower = lax.linalg.triangular_solve(
        lower, jnp.eye(K, dtype=jnp.float32), left_side=True, lower=True
    )
    basis = jnp.sqrt(count) * jnp.einsum(
        "ji,ioc->joc", inverse_lower, sketch_image, precision=highest
    )
    intersection = by_axis(jnp.einsum("ioc,joc->ij", basis, test, precision=highest), TILE) / count
    remainder = test - jnp.einsum("ij,ioc->joc", intersection, basis, precision=highest)
    images = apply_operator(jnp.concatenate([basis, remainder], axis=0))
    image_q = images[:K]
    image_w = images[K:]
    trace_q, trace_w = (
        by_axis(jnp.sum(basis * image_q), TILE),
        by_axis(jnp.sum(remainder * image_w), TILE),
    )
    trace_mean = trace_q / (count * count) + trace_w / (K * count)
    sketch_rayleigh = trace_q / (K * count)
    return (image_q, image_w, trace_mean, sketch_rayleigh)


def solution(mesh):
    finer = Mesh(mesh.devices.reshape(mesh.shape["mem"], 4, 4), ("mem", "tile_0", "tile_1"))
    return jax.shard_map(
        on_device,
        mesh=finer,
        in_specs=(
            P("mem", None, TILE),
            P(),
            P(TILE, None, None),
            P(None, TILE, None),
            P(None, TILE, None),
            P(TILE),
            P(TILE),
        ),
        out_specs=(P(None, TILE, None), P(None, TILE, None), P(), P()),
        check_vma=False,
    )
```

profile of v0, /device:TPU:0, one launch (start us, length us, event | category | flops | bytes accessed | tf_op | source)
XLA Modules:
  0.0 431.1 jit_solution(6855449706677383312)
XLA Ops:
  0.6 13.3 %copy.96 = bf16[128,231,137]{1,2,0:T(8,128)(2,1)} copy(bf16[128,231,137]{0,1,2:T(8,128)(2,1)} %param.13) | data formatting | bytes 16203264 | tf_op args[2]
  14.2 6.2 %fusion.179 = bf16[3,137,128]{1,0,2:T(4,128)(2,1)S(1)} fusion(bf16[3,128,231]{2,0,1:T(4,128)(2,1)S(1)} %copy.95, bf16[128,231,137]{1,2,0:T(8,128)(2,1)} %copy.96), kind=kOutput, calls=%fused_computation.270 | convolution fusion | flops 24357504 | bytes 8384256 | tf_op jit(solution)/shard_map/ocl,poc->plo/dot_general | solution.py:129
  22.1 8.2 %all-to-all-start = ((bf16[411,16,32]{0,2,1:T(8,128)(2,1)}), bf16[411,16,32]{0,2,1:T(8,128)(2,1)S(1)}, u32[]{:S(2)}, u32[]{:S(2)}) async-start(bf16[411,16,32]{0,2,1:T(8,128)(2,1)} %bitcast.5), calls=%async_computation | async-start | bytes 1048576 | tf_op jit(solution)/shard_map/all_to_all | solution.py:138
  30.2 25.7 %all_gather.3 = s32[2048,2]{0,1:T(2,128)S(1)} all-gather(s32[128,2]{0,1:T(2,128)S(1)} %pad_add_fusion), channel_id=1, replica_groups=mesh['mem'=8,'tile_0'=4,'tile_1'=4] {'tile_0','tile_1'}, dimensions={0}, use_global_device_ids=true | all-gather | bytes 17408 | tf_op jit(solution)/shard_map/all_gather | solution.py:33
  56.1 8.0 %scatter_custom_fusion = s32[512]{0:T(512)S(1)} fusion(s32[2048]{0:T(1024)S(1)} %bitcast.110, s32[2048]{0:T(1024)S(1)} %add_select_fusion.12, s32[]{:T(128)} %constant.386.clone.1), kind=kCustom, calls=%fused_computation.340 | custom fusion | bytes 2052 | tf_op jit(solution)/shard_map/scatter | solution.py:117
  64.3 9.1 %scatter_custom_fusion.1 = pred[512]{0:T(512)(128)(4,1)S(1)} fusion(s32[2048]{0:T(1024)S(1)} %bitcast.111, pred[2048]{0:T(1024)(128)(4,1)S(1)} %broadcast.1456, pred[]{:T(512)} %constant.400.clone.1), kind=kCustom, calls=%fused_computation.342 | custom fusion | bytes 513 | tf_op jit(solution)/shard_map/scatter | solution.py:119
  75.1 1.9 fusion.183
  77.0 49.0 %while.32 = (s32[]{:T(128)}, f32[3,137,512]{2,1,0:T(8,128)S(1)}, bf16[2,137,512]{2,1,0:T(8,128)(2,1)S(1)}, f32[3,137,512]{2,1,0:T(8,128)S(1)}, bf16[137,137]{1,0:T(8,128)(2,1)S(1)}, /*index=5*/s32[]{:T(128)}, s32[]{:T(128)}) while((s32[]{:T(128)}, f32[3,137,512]{2,1,0:T(8,128)S(1)}, bf16[2,137,512]{2,1,0:T(8,128)(2,1)S(1)}, ...), condition=%wide.region_3.4_spmd.clone, body=%wide.region_2.3_spmd.clone.sunk | while | flops 77786176 | bytes 52359552 | solution.py:151
  78.9 2.1 collective-permute-start
  81.0 6.5 %collective-permute-done = f32[3,137,192]{2,1,0:T(8,128)} collective-permute-done((f32[3,137,192]{2,1,0:T(8,128)}, f32[3,137,192]{2,1,0:T(8,128)}, u32[]{:S(2)}, u32[]{:S(2)}) %collective-permute-start) | collective-permute-done | bytes 315680 | tf_op jit(solution)/shard_map/while/body/eval_jaxpr/ppermute | solution.py:24
  87.5 5.2 %collective-permute-done.1 = f32[3,137,192]{2,1,0:T(8,128)} collective-permute-done((f32[3,137,192]{2,1,0:T(8,128)S(1)}, f32[3,137,192]{2,1,0:T(8,128)}, u32[]{:S(2)}, u32[]{:S(2)}) %collective-permute-start.1) | collective-permute-done | bytes 315680 | tf_op jit(solution)/shard_map/while/body/eval_jaxpr/ppermute | solution.py:21
  92.7 1.6 pad_maximum_fusion.5
  94.3 1.7 fusion.266
  104.5 1.8 collective-permute-start.1
  106.4 6.5 %collective-permute-done = f32[3,137,192]{2,1,0:T(8,128)} collective-permute-done((f32[3,137,192]{2,1,0:T(8,128)}, f32[3,137,192]{2,1,0:T(8,128)}, u32[]{:S(2)}, u32[]{:S(2)}) %collective-permute-start) | collective-permute-done | bytes 315680 | tf_op jit(solution)/shard_map/while/body/eval_jaxpr/ppermute | solution.py:24
  112.9 3.3 collective-permute-done.1
  117.9 1.7 fusion.266
  127.1 1.6 gather_fusion
  129.5 20.5 %all_to_all.48 = f32[8,411,16,4]{1,3,2,0:T(4,128)S(1)} all-to-all(f32[8,411,16,4]{1,3,2,0:T(4,128)S(1)} %copy.102), channel_id=1, replica_groups=mesh['mem'=8,'tile_0'=4,'tile_1'=4] {'mem'}, dimensions={0} | all-to-all | bytes 1683456 | tf_op jit(solution)/shard_map/all_to_all | solution.py:50
  150.3 10.2 %all_to_all.49 = bf16[411,16,4]{0,2,1:T(4,128)(2,1)S(1)} all-to-all(bf16[411,16,4]{0,2,1:T(4,128)(2,1)S(1)} %multiply_convert_fusion.5), channel_id=1, replica_groups=mesh['mem'=8,'tile_0'=4,'tile_1'=4] {'tile_0','tile_1'}, dimensions={1} | all-to-all | bytes 105216 | tf_op jit(solution)/shard_map/all_to_all | solution.py:159
  160.6 12.8 %all_to_all.50 = bf16[8,411,16,4]{1,3,2,0:T(4,128)(2,1)S(1)} all-to-all(bf16[8,411,16,4]{1,3,2,0:T(4,128)(2,1)S(1)} %broadcast_in_dim.146), channel_id=1, replica_groups=mesh['mem'=8,'tile_0'=4,'tile_1'=4] {'mem'}, dimensions={0} | all-to-all | bytes 841728 | tf_op jit(solution)/shard_map/all_to_all | solution.py:56
  174.5 5.0 %convolution_bitcast_fusion.2 = f32[3,128,231]{2,0,1:T(4,128)S(1)} fusion(bf16[3,137,128]{1,0,2:T(4,128)(2,1)S(1)} %copy.104, bf16[128,231,137]{1,2,0:T(8,128)(2,1)} %copy.96), kind=kOutput, calls=%fused_computation.267 | convolution fusion | flops 24304896 | bytes 8561664 | tf_op jit(solution)/shard_map/ocl,plo->poc/dot_general | solution.py:166
  179.6 2.3 convolution_bitcast_fusion.5
  182.0 8.8 %psum.56 = f32[3,3]{0,1:T(4,128)S(1)} all-reduce(f32[3,3]{0,1:T(4,128)S(1)} %convolution_bitcast_fusion.5), channel_id=1, replica_groups=mesh['mem'=8,'tile_0'=4,'tile_1'=4] {'tile_0'}, use_global_device_ids=true, to_apply=%region_5.6 | all-reduce | flops 9 | bytes 72 | tf_op jit(solution)/shard_map/psum | solution.py:74
  191.1 8.9 %psum.57 = f32[3,3]{0,1:T(4,128)S(1)} all-reduce(f32[3,3]{0,1:T(4,128)S(1)} %psum.56), channel_id=1, replica_groups=mesh['mem'=8,'tile_0'=4,'tile_1'=4] {'tile_1'}, use_global_device_ids=true, to_apply=%region_6.7 | all-reduce | flops 9 | bytes 72 | tf_op jit(solution)/shard_map/psum | solution.py:74
  203.2 2.2 convolution_bitcast_fusion.3
  205.4 8.6 %psum.58 = f32[3,3]{1,0:T(4,128)S(1)} all-reduce(f32[3,3]{1,0:T(4,128)S(1)} %convolution_bitcast_fusion.3), channel_id=1, replica_groups=mesh['mem'=8,'tile_0'=4,'tile_1'=4] {'tile_0'}, use_global_device_ids=true, to_apply=%region_9.10 | all-reduce | flops 9 | bytes 72 | tf_op jit(solution)/shard_map/psum | solution.py:74
  214.0 8.6 %psum.59 = f32[3,3]{1,0:T(4,128)S(1)} all-reduce(f32[3,3]{1,0:T(4,128)S(1)} %psum.58), channel_id=1, replica_groups=mesh['mem'=8,'tile_0'=4,'tile_1'=4] {'tile_1'}, use_global_device_ids=true, to_apply=%region_10.11 | all-reduce | flops 9 | bytes 72 | tf_op jit(solution)/shard_map/psum | solution.py:74
  224.3 6.2 %fusion.178 = bf16[6,137,128]{1,0,2:T(8,128)(2,1)S(1)} fusion(bf16[6,128,231]{2,0,1:T(8,128)(2,1)S(1)} %copy.116, bf16[128,231,137]{1,2,0:T(8,128)(2,1)} %copy.96), kind=kOutput, calls=%fused_computation.266 | convolution fusion | flops 48715008 | bytes 8666880 | tf_op jit(solution)/shard_map/ocl,poc->plo/dot_general | solution.py:129
  232.7 3.6 all-to-all-start.4
  236.3 12.4 %all-to-all-done.4 = bf16[822,16,32]{0,2,1:T(8,128)(2,1)S(1)} async-done(((bf16[822,16,32]{0,2,1:T(8,128)(2,1)}), bf16[822,16,32]{0,2,1:T(8,128)(2,1)S(1)}, u32[]{:S(2)}, u32[]{:S(2)}) %all-to-all-start.4) | async-done | bytes 841760 | tf_op jit(solution)/shard_map/all_to_all | solution.py:138
  248.7 3.1 dot_general.78
  251.8 3.8 fusion.176
  255.6 79.9 %while.33 = (s32[]{:T(128)}, f32[6,137,512]{2,1,0:T(8,128)}, bf16[2,137,512]{2,1,0:T(8,128)(2,1)S(1)}, f32[6,137,512]{2,1,0:T(8,128)}, bf16[137,137]{1,0:T(8,128)(2,1)S(1)}, /*index=5*/s32[]{:T(128)}, s32[]{:T(128)}) while((s32[]{:T(128)}, f32[6,137,512]{2,1,0:T(8,128)}, bf16[2,137,512]{2,1,0:T(8,128)(2,1)S(1)}, ...), condition=%wide.region_12.13_spmd.clone, body=%wide.region_11.12_spmd.clone.sunk | while | flops 155461888 | bytes 112613240 | solution.py:151
  255.8 2.0 convolution_bitcast_fusion.9
  261.1 11.3 %collective-permute-done.2 = f32[6,137,192]{2,1,0:T(8,128)} collective-permute-done((f32[6,137,192]{2,1,0:T(8,128)}, f32[6,137,192]{2,1,0:T(8,128)}, u32[]{:S(2)}, u32[]{:S(2)}) %collective-permute-start.2) | collective-permute-done | bytes 631328 | tf_op jit(solution)/shard_map/while/body/eval_jaxpr/ppermute | solution.py:24
  272.4 4.3 collective-permute-done.3
  276.7 2.3 pad_maximum_fusion.6
  279.0 3.4 fusion.280
  282.4 2.8 fusion.282
  285.2 2.8 fusion.284
  288.0 2.3 fusion.286
  290.4 2.3 fusion.288
  292.7 2.1 fusion.290
  296.1 2.0 convolution_bitcast_fusion.9
  299.5 1.8 collective-permute-start.3
  301.4 11.3 %collective-permute-done.2 = f32[6,137,192]{2,1,0:T(8,128)} collective-permute-done((f32[6,137,192]{2,1,0:T(8,128)}, f32[6,137,192]{2,1,0:T(8,128)}, u32[]{:S(2)}, u32[]{:S(2)}) %collective-permute-start.2) | collective-permute-done | bytes 631328 | tf_op jit(solution)/shard_map/while/body/eval_jaxpr/ppermute | solution.py:24
  312.7 3.3 collective-permute-done.3
  316.0 2.3 pad_maximum_fusion.6
  318.3 3.4 fusion.280
  321.7 2.8 fusion.282
  324.5 2.8 fusion.284
  327.3 2.3 fusion.286
  329.6 2.3 fusion.288
  332.0 2.1 fusion.290
  335.5 1.8 reshape.300
  338.1 2.6 gather_fusion.1
  340.7 1.8 gather.15
  343.3 26.8 %all_to_all.51 = f32[8,822,16,4]{1,3,2,0:T(4,128)S(1)} all-to-all(f32[8,822,16,4]{1,3,2,0:T(4,128)S(1)} %copy.123), channel_id=1, replica_groups=mesh['mem'=8,'tile_0'=4,'tile_1'=4] {'mem'}, dimensions={0} | all-to-all | bytes 3366912 | tf_op jit(solution)/shard_map/all_to_all | solution.py:50
  370.6 10.5 %all_to_all.52 = bf16[822,16,4]{0,2,1:T(4,128)(2,1)S(1)} all-to-all(bf16[822,16,4]{0,2,1:T(4,128)(2,1)S(1)} %multiply_convert_fusion.4), channel_id=1, replica_groups=mesh['mem'=8,'tile_0'=4,'tile_1'=4] {'tile_0','tile_1'}, dimensions={1} | all-to-all | bytes 210432 | tf_op jit(solution)/shard_map/all_to_all | solution.py:159
  381.4 17.0 %all_to_all.53 = bf16[8,822,16,4]{1,3,2,0:T(4,128)(2,1)S(1)} all-to-all(bf16[8,822,16,4]{1,3,2,0:T(4,128)(2,1)S(1)} %broadcast_in_dim.148), channel_id=1, replica_groups=mesh['mem'=8,'tile_0'=4,'tile_1'=4] {'mem'}, dimensions={0} | all-to-all | bytes 1683456 | tf_op jit(solution)/shard_map/all_to_all | solution.py:56
  400.1 5.0 %fusion.218 = f32[128,6,231]{2,1,0:T(8,128)S(1)} fusion(bf16[6,137,128]{1,0,2:T(8,128)(2,1)S(1)} %copy.125, bf16[128,231,137]{1,2,0:T(8,128)(2,1)} %copy.96), kind=kOutput, calls=%fused_computation.351 | convolution fusion | flops 48609792 | bytes 9021696 | tf_op jit(solution)/shard_map/ocl,plo->poc/dot_general | solution.py:166
  407.9 9.2 %all-reduce.1 = (f32[]{:T(128)}, f32[]{:T(128)}) all-reduce(f32[]{:T(128)} %get-tuple-element.418, f32[]{:T(128)} %get-tuple-element.384), channel_id=1, replica_groups=mesh['mem'=8,'tile_0'=4,'tile_1'=4] {'tile_0'}, use_global_device_ids=true, to_apply=%region_15.16 | all-reduce | flops 2 | bytes 16 | tf_op jit(solution)/shard_map/psum | solution.py:74
  417.1 9.6 %all-reduce = (f32[]{:T(128)}, f32[]{:T(128)}) all-reduce(f32[]{:T(128)} %get-tuple-element.382, f32[]{:T(128)} %get-tuple-element.383), channel_id=1, replica_groups=mesh['mem'=8,'tile_0'=4,'tile_1'=4] {'tile_1'}, use_global_device_ids=true, to_apply=%region_16.17 | all-reduce | flops 2 | bytes 16 | tf_op jit(solution)/shard_map/psum | solution.py:74
  (168 shorter events, 46.6 us)
Async XLA Ops:
  0.6 13.3 %copy-start.13 = (s32[3,128,231]{1,2,0:T(8,128)S(1)}, s32[3,128,231]{1,2,0:T(8,128)}, u32[]{:S(2)}) copy-start(s32[3,128,231]{1,2,0:T(8,128)} %param.14) | copy-start | bytes 1064452
  14.2 6.4 %copy-start.21 = (s32[128]{0:T(128)S(1)}, s32[128]{0:T(128)}, u32[]{:S(2)}) copy-start(s32[128]{0:T(128)} %param.17) | copy-start | bytes 1540
  14.2 6.4 %copy-start.22 = (s32[128]{0:T(128)S(1)}, s32[128]{0:T(128)}, u32[]{:S(2)}) copy-start(s32[128]{0:T(128)} %param.16) | copy-start | bytes 1540
  20.4 43.7 %copy-start.14 = (bf16[2,137,512]{2,0,1:T(2,128)(2,1)S(1)}, bf16[2,137,512]{2,0,1:T(2,128)(2,1)}, u32[]{:S(2)}) copy-start(bf16[2,137,512]{2,0,1:T(2,128)(2,1)} %param.11) | copy-start | bytes 841732
  20.7 210.2 %copy-start.19 = (s32[128]{0:T(128)}, s32[128]{0:T(128)S(1)}, u32[]{:S(2)}) copy-start(s32[128]{0:T(128)S(1)} %multiply_add_fusion) | copy-start | bytes 1540
  22.1 51.5 %all-to-all-start = ((bf16[411,16,32]{0,2,1:T(8,128)(2,1)}), bf16[411,16,32]{0,2,1:T(8,128)(2,1)S(1)}, u32[]{:S(2)}, u32[]{:S(2)}) async-start(bf16[411,16,32]{0,2,1:T(8,128)(2,1)} %bitcast.5), calls=%async_computation | async-start | bytes 1048576 | tf_op jit(solution)/shard_map/all_to_all | solution.py:138
  64.3 64.8 %copy-start.15 = (pred[16,8,4]{2,1,0:T(8,128)(4,1)}, pred[16,8,4]{2,1,0:T(8,128)(4,1)S(1)}, u32[]{:S(2)}) copy-start(pred[16,8,4]{2,1,0:T(8,128)(4,1)S(1)} %broadcast_in_dim.137) | copy-start | bytes 1540
  73.5 53.6 %copy-start.17 = (s32[1024]{0:T(1024)}, s32[1024]{0:T(1024)S(1)}, u32[]{:S(2)}) copy-start(s32[1024]{0:T(1024)S(1)} %pad_clamp_fusion) | copy-start | bytes 12292
  73.5 3.5 copy-start.8
  77.0 0.7 copy-start.2
  78.9 8.6 %collective-permute-start = (f32[3,137,192]{2,1,0:T(8,128)}, f32[3,137,192]{2,1,0:T(8,128)}, u32[]{:S(2)}, u32[]{:S(2)}) collective-permute-start(f32[3,137,192]{2,1,0:T(8,128)} %get-tuple-element.507), channel_id=1, source_target_pairs={{1,0},{2,1},{3,2},{4,3},{5,4},{6,5},{7,6},{8,7},{9,8},{10,9},{11,1... | collective-permute-start | bytes 946952 | tf_op jit(solution)/shard_map/while/body/eval_jaxpr/ppermute | solution.py:24
  81.0 11.7 %collective-permute-start.1 = (f32[3,137,192]{2,1,0:T(8,128)S(1)}, f32[3,137,192]{2,1,0:T(8,128)}, u32[]{:S(2)}, u32[]{:S(2)}) collective-permute-start(f32[3,137,192]{2,1,0:T(8,128)S(1)} %get-tuple-element.508), channel_id=1, source_target_pairs={{0,1},{1,2},{2,3},{3,4},{4,5},{5,6},{6,7},{7,8},{8,9},{9,10},{10,1... | collective-permute-start | bytes 946952 | tf_op jit(solution)/shard_map/while/body/eval_jaxpr/ppermute | solution.py:21
  101.3 1.1 copy-start.3
  102.4 0.7 copy-start.2
  104.3 8.6 %collective-permute-start = (f32[3,137,192]{2,1,0:T(8,128)}, f32[3,137,192]{2,1,0:T(8,128)}, u32[]{:S(2)}, u32[]{:S(2)}) collective-permute-start(f32[3,137,192]{2,1,0:T(8,128)} %get-tuple-element.507), channel_id=1, source_target_pairs={{1,0},{2,1},{3,2},{4,3},{5,4},{6,5},{7,6},{8,7},{9,8},{10,9},{11,1... | collective-permute-start | bytes 946952 | tf_op jit(solution)/shard_map/while/body/eval_jaxpr/ppermute | solution.py:24
  104.5 11.7 %collective-permute-start.1 = (f32[3,137,192]{2,1,0:T(8,128)S(1)}, f32[3,137,192]{2,1,0:T(8,128)}, u32[]{:S(2)}, u32[]{:S(2)}) collective-permute-start(f32[3,137,192]{2,1,0:T(8,128)S(1)} %get-tuple-element.508), channel_id=1, source_target_pairs={{0,1},{1,2},{2,3},{3,4},{4,5},{5,6},{6,7},{7,8},{8,9},{9,10},{10,1... | collective-permute-start | bytes 946952 | tf_op jit(solution)/shard_map/while/body/eval_jaxpr/ppermute | solution.py:21
  124.8 1.1 copy-start.3
  125.9 0.7 copy-start.4
  174.5 7.4 %copy-start.11 = (s32[3,128,231]{1,2,0:T(8,128)S(1)}, s32[3,128,231]{1,2,0:T(8,128)}, u32[]{:S(2)}) copy-start(s32[3,128,231]{1,2,0:T(8,128)} %param.15) | copy-start | bytes 1064452
  203.2 20.7 %copy-start.6 = (f32[3,128,231]{1,2,0:T(8,128)}, f32[3,128,231]{1,2,0:T(8,128)S(1)}, u32[]{:S(2)}) copy-start(f32[3,128,231]{1,2,0:T(8,128)S(1)} %get-tuple-element.389) | copy-start | bytes 1064452
  223.7 6.8 %copy-start.9 = (f32[3,128,231]{1,0,2:T(4,128)}, f32[3,128,231]{1,0,2:T(4,128)S(1)}, u32[]{:S(2)}) copy-start(f32[3,128,231]{1,0,2:T(4,128)S(1)} %fusion.190) | copy-start | bytes 1064452
  232.7 16.1 %all-to-all-start.4 = ((bf16[822,16,32]{0,2,1:T(8,128)(2,1)}), bf16[822,16,32]{0,2,1:T(8,128)(2,1)S(1)}, u32[]{:S(2)}, u32[]{:S(2)}) async-start(bf16[822,16,32]{0,2,1:T(8,128)(2,1)} %bitcast.19), calls=%async_computation.4 | async-start | bytes 1835008 | tf_op jit(solution)/shard_map/all_to_all | solution.py:138
  251.8 3.8 copy-start.5
  259.0 13.4 %collective-permute-start.2 = (f32[6,137,192]{2,1,0:T(8,128)}, f32[6,137,192]{2,1,0:T(8,128)}, u32[]{:S(2)}, u32[]{:S(2)}) collective-permute-start(f32[6,137,192]{2,1,0:T(8,128)} %get-tuple-element.526), channel_id=1, source_target_pairs={{1,0},{2,1},{3,2},{4,3},{5,4},{6,5},{7,6},{8,7},{9,8},{10,9},{11,1... | collective-permute-start | bytes 1893896 | tf_op jit(solution)/shard_map/while/body/eval_jaxpr/ppermute | solution.py:24
  260.2 16.5 %collective-permute-start.3 = (f32[6,137,192]{2,1,0:T(8,128)S(1)}, f32[6,137,192]{2,1,0:T(8,128)}, u32[]{:S(2)}, u32[]{:S(2)}) collective-permute-start(f32[6,137,192]{2,1,0:T(8,128)S(1)} %get-tuple-element.527), channel_id=1, source_target_pairs={{0,1},{1,2},{2,3},{3,4},{4,5},{5,6},{6,7},{7,8},{8,9},{9,10},{10,1... | collective-permute-start | bytes 1893896 | tf_op jit(solution)/shard_map/while/body/eval_jaxpr/ppermute | solution.py:21
  290.4 2.4 copy-start
  294.8 1.2 copy-start.1
  299.3 13.4 %collective-permute-start.2 = (f32[6,137,192]{2,1,0:T(8,128)}, f32[6,137,192]{2,1,0:T(8,128)}, u32[]{:S(2)}, u32[]{:S(2)}) collective-permute-start(f32[6,137,192]{2,1,0:T(8,128)} %get-tuple-element.526), channel_id=1, source_target_pairs={{1,0},{2,1},{3,2},{4,3},{5,4},{6,5},{7,6},{8,7},{9,8},{10,9},{11,1... | collective-permute-start | bytes 1893896 | tf_op jit(solution)/shard_map/while/body/eval_jaxpr/ppermute | solution.py:24
  299.5 16.5 %collective-permute-start.3 = (f32[6,137,192]{2,1,0:T(8,128)S(1)}, f32[6,137,192]{2,1,0:T(8,128)}, u32[]{:S(2)}, u32[]{:S(2)}) collective-permute-start(f32[6,137,192]{2,1,0:T(8,128)S(1)} %get-tuple-element.527), channel_id=1, source_target_pairs={{0,1},{1,2},{2,3},{3,4},{4,5},{5,6},{6,7},{7,8},{8,9},{9,10},{10,1... | collective-permute-start | bytes 1893896 | tf_op jit(solution)/shard_map/while/body/eval_jaxpr/ppermute | solution.py:21
  329.6 2.4 copy-start
  334.1 1.2 copy-start.1
  337.3 0.8 copy-start.18
  340.7 1.9 copy-start.16
  398.3 0.8 copy-start.20
  405.1 1.0 copy-start.7
  405.1 1.1 copy-start.10
  405.1 1.2 copy-start.12
where the time goes:
time: 439 us; the launch traced here: 431 us
  blocking collectives  177 us (40%)
  waiting for transfers between devices  64.1 us (15%)
  local copies, waits for them, and re-layouts  61.2 us (14%)
  other arithmetic  60.9 us (14%)
  matrix products  41.2 us (9%)
  starting transfers between devices  19.9 us (5%)
  between operations  5.68 us (1%)
    psum x6, blocking collectives, by_axis(): value = lax.psum(value, axis)  53.8 us
    all_to_all x2, blocking collectives, sum_at_owner(): lax.all_to_all(pieces, axis, split_axis=0, concat_axis=0, tiled=True)  47.3 us
    add x20, other arithmetic, relax(): center + diffusion_rate * (north - center + (south - center) + west_ok *...  41.3 us
    ppermute x4, waiting for transfers between devices, with_halo(): lax.ppermute(lax.slice_in_dim(block, 0, width, axis=dim), axis, backward)  35.6 us
    all_to_all x2, blocking collectives, from_everyone(): lax.all_to_all(jnp.broadcast_to(value[None], (peers, *value.shape)), axis...  29.7 us
    all_gather x1, blocking collectives, gather_turned(): whole = lax.all_gather(both, axis, axis=0, tiled=True)  25.7 us
    all_to_all x2, blocking collectives, apply_operator(): lax.all_to_all(outbound, TILE, split_axis=1, concat_axis=1, tiled=True)  20.7 us
    ppermute x4, waiting for transfers between devices, with_halo(): lax.ppermute(lax.slice_in_dim(block, block.shape[dim] - width, None, axis...  16.1 us
  transfers between devices with their start and end apart: 10, of which 9 were waited for; matrix products, arithmetic and copies ran while one was open for 4% of the time, Pallas kernels for 0%

commit v1 on v0

--- a/solution.py
+++ b/solution.py
@@ -135,7 +135,15 @@
         outgoing = jnp.dot(
             adjoint.reshape(rows, obs_local), collect, preferred_element_type=jnp.float32
         ).astype(jnp.bfloat16)
-        arrived = lax.all_to_all(outgoing, TILE, split_axis=1, concat_axis=1, tiled=True)
+        arrived = jnp.concatenate(
+            lax.all_to_all(
+                jnp.stack(jnp.split(outgoing, lax.psum(1, axis_name=TILE), 1), 0),
+                axis_name=TILE,
+                split_axis=0,
+                concat_axis=0,
+            ),
+            1,
+        )
         field_sum = jnp.dot(arrived, spread, preferred_element_type=jnp.float32).reshape(
             probes, levels, cell_count
         )

time: 439 us -> 464 us (1.057)
  local copies, waits for them, and re-layouts: 61.2 us -> 85.2 us
    unnamed x40 -> x70, local copies, waits for them, and re-layouts: 15 us -> 33.4 us
    another operation x0 -> x36, local copies, waits for them, and re-layouts: none -> 7.55 us  [apply_operator(): jnp.stack(jnp.split(outgoing, lax.psum(1, axis_name=TILE), 1), 0)]
where the time goes in v1:
time: 464 us; the launch traced here: 455 us
  blocking collectives  177 us (38%)
  local copies, waits for them, and re-layouts  85.2 us (18%)
  waiting for transfers between devices  64.1 us (14%)
  other arithmetic  60.9 us (13%)
  matrix products  41.2 us (9%)
  starting transfers between devices  19.9 us (4%)
  between operations  5.84 us (1%)
    psum x6, blocking collectives, by_axis(): value = lax.psum(value, axis)  53.8 us
    all_to_all x2, blocking collectives, sum_at_owner(): lax.all_to_all(pieces, axis, split_axis=0, concat_axis=0, tiled=True)  47.1 us
    add x20, other arithmetic, relax(): center + diffusion_rate * (north - center + (south - center) + west_ok *...  41.3 us
    ppermute x4, waiting for transfers between devices, with_halo(): lax.ppermute(lax.slice_in_dim(block, 0, width, axis=dim), axis, backward)  35.6 us
    unnamed x70, local copies, waits for them, and re-layouts  33.4 us
    all_to_all x2, blocking collectives, from_everyone(): lax.all_to_all(jnp.broadcast_to(value[None], (peers, *value.shape)), axis...  29.7 us
    all_gather x1, blocking collectives, gather_turned(): whole = lax.all_gather(both, axis, axis=0, tiled=True)  25.7 us
    all_to_all x2, blocking collectives, apply_operator(): lax.all_to_all(outbound, TILE, split_axis=1, concat_axis=1, tiled=True)  20.7 us
  transfers between devices with their start and end apart: 10, of which 9 were waited for; matrix products, arithmetic and copies ran while one was open for 4% of the time, Pallas kernels for 0%

profile of v1, /device:TPU:0, one launch (start us, length us, event | category | flops | bytes accessed | tf_op | source)
XLA Modules:
  0.0 455.2 jit_solution(17265314785735336314)
XLA Ops:
  0.6 13.2 %copy.126 = bf16[128,231,137]{1,2,0:T(8,128)(2,1)} copy(bf16[128,231,137]{0,1,2:T(8,128)(2,1)} %param.13) | data formatting | bytes 16203264 | tf_op args[2]
  14.1 6.2 %fusion.179 = bf16[3,137,128]{1,0,2:T(4,128)(2,1)S(1)} fusion(bf16[3,128,231]{2,0,1:T(4,128)(2,1)S(1)} %copy.125, bf16[128,231,137]{1,2,0:T(8,128)(2,1)} %copy.126), kind=kOutput, calls=%fused_computation.270 | convolution fusion | flops 24357504 | bytes 8384256 | tf_op jit(solution)/shard_map/ocl,poc->plo/dot_general | solution.py:129
  32.7 8.2 %all-to-all-start = ((bf16[16,411,32]{1,2,0:T(8,128)(2,1)}), bf16[16,411,32]{1,2,0:T(8,128)(2,1)S(1)}, u32[]{:S(2)}, u32[]{:S(2)}) async-start(bf16[16,411,32]{1,2,0:T(8,128)(2,1)} %constant_dynamic-update-slice_fusion), calls=%async_computation | async-start | bytes 1048576 | tf_op jit(solution)/shard_map/all_to_all | solution.py:139
  40.9 25.7 %all_gather.3 = s32[2048,2]{0,1:T(2,128)S(1)} all-gather(s32[128,2]{0,1:T(2,128)S(1)} %pad_add_fusion), channel_id=1, replica_groups=mesh['mem'=8,'tile_0'=4,'tile_1'=4] {'tile_0','tile_1'}, dimensions={0}, use_global_device_ids=true | all-gather | bytes 17408 | tf_op jit(solution)/shard_map/all_gather | solution.py:33
  66.7 8.0 %scatter_custom_fusion = s32[512]{0:T(512)S(1)} fusion(s32[2048]{0:T(1024)S(1)} %bitcast.176, s32[2048]{0:T(1024)S(1)} %add_select_fusion.12, s32[]{:T(128)} %constant.386.clone.1), kind=kCustom, calls=%fused_computation.404 | custom fusion | bytes 2052 | tf_op jit(solution)/shard_map/scatter | solution.py:117
  75.0 9.1 %scatter_custom_fusion.1 = pred[512]{0:T(512)(128)(4,1)S(1)} fusion(s32[2048]{0:T(1024)S(1)} %bitcast.177, pred[2048]{0:T(1024)(128)(4,1)S(1)} %broadcast.1456, pred[]{:T(512)} %constant.400.clone.1), kind=kCustom, calls=%fused_computation.406 | custom fusion | bytes 513 | tf_op jit(solution)/shard_map/scatter | solution.py:119
  84.1 1.9 dot_general.68
  86.0 1.9 fusion.183
  87.9 49.0 %while.32 = (s32[]{:T(128)}, f32[3,137,512]{2,1,0:T(8,128)S(1)}, bf16[2,137,512]{2,1,0:T(8,128)(2,1)S(1)}, f32[3,137,512]{2,1,0:T(8,128)S(1)}, bf16[137,137]{1,0:T(8,128)(2,1)S(1)}, /*index=5*/s32[]{:T(128)}, s32[]{:T(128)}) while((s32[]{:T(128)}, f32[3,137,512]{2,1,0:T(8,128)S(1)}, bf16[2,137,512]{2,1,0:T(8,128)(2,1)S(1)}, ...), condition=%wide.region_3.4_spmd.clone, body=%wide.region_2.3_spmd.clone.sunk | while | flops 77786176 | bytes 52359552 | solution.py:159
  89.8 2.1 collective-permute-start
  91.9 6.5 %collective-permute-done = f32[3,137,192]{2,1,0:T(8,128)} collective-permute-done((f32[3,137,192]{2,1,0:T(8,128)}, f32[3,137,192]{2,1,0:T(8,128)}, u32[]{:S(2)}, u32[]{:S(2)}) %collective-permute-start) | collective-permute-done | bytes 315680 | tf_op jit(solution)/shard_map/while/body/eval_jaxpr/ppermute | solution.py:24
  98.4 5.2 %collective-permute-done.1 = f32[3,137,192]{2,1,0:T(8,128)} collective-permute-done((f32[3,137,192]{2,1,0:T(8,128)S(1)}, f32[3,137,192]{2,1,0:T(8,128)}, u32[]{:S(2)}, u32[]{:S(2)}) %collective-permute-start.1) | collective-permute-done | bytes 315680 | tf_op jit(solution)/shard_map/while/body/eval_jaxpr/ppermute | solution.py:21
  105.2 1.7 fusion.266
  115.4 1.8 collective-permute-start.1
  117.3 6.5 %collective-permute-done = f32[3,137,192]{2,1,0:T(8,128)} collective-permute-done((f32[3,137,192]{2,1,0:T(8,128)}, f32[3,137,192]{2,1,0:T(8,128)}, u32[]{:S(2)}, u32[]{:S(2)}) %collective-permute-start) | collective-permute-done | bytes 315680 | tf_op jit(solution)/shard_map/while/body/eval_jaxpr/ppermute | solution.py:24
  123.8 3.3 collective-permute-done.1
  128.8 1.7 fusion.266
  138.0 1.6 gather_fusion
  140.4 20.2 %all_to_all.40 = f32[8,411,16,4]{1,3,2,0:T(4,128)S(1)} all-to-all(f32[8,411,16,4]{1,3,2,0:T(4,128)S(1)} %copy.147), channel_id=1, replica_groups=mesh['mem'=8,'tile_0'=4,'tile_1'=4] {'mem'}, dimensions={0} | all-to-all | bytes 1683456 | tf_op jit(solution)/shard_map/all_to_all | solution.py:50
  160.9 10.2 %all_to_all.41 = bf16[411,16,4]{0,2,1:T(4,128)(2,1)S(1)} all-to-all(bf16[411,16,4]{0,2,1:T(4,128)(2,1)S(1)} %multiply_convert_fusion.5), channel_id=1, replica_groups=mesh['mem'=8,'tile_0'=4,'tile_1'=4] {'tile_0','tile_1'}, dimensions={1} | all-to-all | bytes 105216 | tf_op jit(solution)/shard_map/all_to_all | solution.py:167
  171.3 12.8 %all_to_all.42 = bf16[8,411,16,4]{1,3,2,0:T(4,128)(2,1)S(1)} all-to-all(bf16[8,411,16,4]{1,3,2,0:T(4,128)(2,1)S(1)} %broadcast_in_dim.146), channel_id=1, replica_groups=mesh['mem'=8,'tile_0'=4,'tile_1'=4] {'mem'}, dimensions={0} | all-to-all | bytes 841728 | tf_op jit(solution)/shard_map/all_to_all | solution.py:56
  185.2 5.0 %convolution_bitcast_fusion.2 = f32[3,128,231]{2,0,1:T(4,128)S(1)} fusion(bf16[3,137,128]{1,0,2:T(4,128)(2,1)S(1)} %copy.149, bf16[128,231,137]{1,2,0:T(8,128)(2,1)} %copy.126), kind=kOutput, calls=%fused_computation.267 | convolution fusion | flops 24304896 | bytes 8561664 | tf_op jit(solution)/shard_map/ocl,plo->poc/dot_general | solution.py:174
  190.2 2.3 convolution_bitcast_fusion.5
  192.7 8.8 %psum.56 = f32[3,3]{0,1:T(4,128)S(1)} all-reduce(f32[3,3]{0,1:T(4,128)S(1)} %convolution_bitcast_fusion.5), channel_id=1, replica_groups=mesh['mem'=8,'tile_0'=4,'tile_1'=4] {'tile_0'}, use_global_device_ids=true, to_apply=%region_5.6 | all-reduce | flops 9 | bytes 72 | tf_op jit(solution)/shard_map/psum | solution.py:74
  201.8 8.9 %psum.57 = f32[3,3]{0,1:T(4,128)S(1)} all-reduce(f32[3,3]{0,1:T(4,128)S(1)} %psum.56), channel_id=1, replica_groups=mesh['mem'=8,'tile_0'=4,'tile_1'=4] {'tile_1'}, use_global_device_ids=true, to_apply=%region_6.7 | all-reduce | flops 9 | bytes 72 | tf_op jit(solution)/shard_map/psum | solution.py:74
  213.9 2.2 convolution_bitcast_fusion.3
  216.1 8.6 %psum.58 = f32[3,3]{1,0:T(4,128)S(1)} all-reduce(f32[3,3]{1,0:T(4,128)S(1)} %convolution_bitcast_fusion.3), channel_id=1, replica_groups=mesh['mem'=8,'tile_0'=4,'tile_1'=4] {'tile_0'}, use_global_device_ids=true, to_apply=%region_9.10 | all-reduce | flops 9 | bytes 72 | tf_op jit(solution)/shard_map/psum | solution.py:74
  224.7 8.6 %psum.59 = f32[3,3]{1,0:T(4,128)S(1)} all-reduce(f32[3,3]{1,0:T(4,128)S(1)} %psum.58), channel_id=1, replica_groups=mesh['mem'=8,'tile_0'=4,'tile_1'=4] {'tile_1'}, use_global_device_ids=true, to_apply=%region_10.11 | all-reduce | flops 9 | bytes 72 | tf_op jit(solution)/shard_map/psum | solution.py:74
  235.0 6.2 %fusion.178 = bf16[6,137,128]{1,0,2:T(8,128)(2,1)S(1)} fusion(bf16[6,128,231]{2,0,1:T(8,128)(2,1)S(1)} %copy.161, bf16[128,231,137]{1,2,0:T(8,128)(2,1)} %copy.126), kind=kOutput, calls=%fused_computation.266 | convolution fusion | flops 48715008 | bytes 8666880 | tf_op jit(solution)/shard_map/ocl,poc->plo/dot_general | solution.py:129
  256.6 3.6 all-to-all-start.4
  260.3 12.4 %all-to-all-done.4 = bf16[16,822,32]{1,2,0:T(8,128)(2,1)S(1)} async-done(((bf16[16,822,32]{1,2,0:T(8,128)(2,1)}), bf16[16,822,32]{1,2,0:T(8,128)(2,1)S(1)}, u32[]{:S(2)}, u32[]{:S(2)}) %all-to-all-start.4) | async-done | bytes 841760 | tf_op jit(solution)/shard_map/all_to_all | solution.py:139
  272.7 3.0 dot_general.78
  275.8 3.8 fusion.176
  279.6 80.0 %while.33 = (s32[]{:T(128)}, f32[6,137,512]{2,1,0:T(8,128)}, bf16[2,137,512]{2,1,0:T(8,128)(2,1)S(1)}, f32[6,137,512]{2,1,0:T(8,128)}, bf16[137,137]{1,0:T(8,128)(2,1)S(1)}, /*index=5*/s32[]{:T(128)}, s32[]{:T(128)}) while((s32[]{:T(128)}, f32[6,137,512]{2,1,0:T(8,128)}, bf16[2,137,512]{2,1,0:T(8,128)(2,1)S(1)}, ...), condition=%wide.region_12.13_spmd.clone, body=%wide.region_11.12_spmd.clone.sunk | while | flops 155461888 | bytes 112613240 | solution.py:159
  280.0 2.0 convolution_bitcast_fusion.9
  285.3 11.3 %collective-permute-done.2 = f32[6,137,192]{2,1,0:T(8,128)} collective-permute-done((f32[6,137,192]{2,1,0:T(8,128)}, f32[6,137,192]{2,1,0:T(8,128)}, u32[]{:S(2)}, u32[]{:S(2)}) %collective-permute-start.2) | collective-permute-done | bytes 631328 | tf_op jit(solution)/shard_map/while/body/eval_jaxpr/ppermute | solution.py:24
  296.6 4.3 collective-permute-done.3
  300.9 2.3 pad_maximum_fusion.6
  303.2 3.4 fusion.280
  306.6 2.8 fusion.282
  309.4 2.8 fusion.284
  312.2 2.3 fusion.286
  314.5 2.3 fusion.288
  316.9 2.1 fusion.290
  320.3 2.0 convolution_bitcast_fusion.9
  323.7 1.8 collective-permute-start.3
  325.5 11.3 %collective-permute-done.2 = f32[6,137,192]{2,1,0:T(8,128)} collective-permute-done((f32[6,137,192]{2,1,0:T(8,128)}, f32[6,137,192]{2,1,0:T(8,128)}, u32[]{:S(2)}, u32[]{:S(2)}) %collective-permute-start.2) | collective-permute-done | bytes 631328 | tf_op jit(solution)/shard_map/while/body/eval_jaxpr/ppermute | solution.py:24
  336.8 3.3 collective-permute-done.3
  340.1 2.3 pad_maximum_fusion.6
  342.4 3.4 fusion.280
  345.8 2.8 fusion.282
  348.6 2.8 fusion.284
  351.4 2.3 fusion.286
  353.8 2.3 fusion.288
  356.2 2.1 fusion.290
  359.7 1.8 reshape.306
  362.2 2.7 gather_fusion.1
  364.9 1.8 gather.15
  367.5 26.8 %all_to_all.43 = f32[8,822,16,4]{1,3,2,0:T(4,128)S(1)} all-to-all(f32[8,822,16,4]{1,3,2,0:T(4,128)S(1)} %copy.183), channel_id=1, replica_groups=mesh['mem'=8,'tile_0'=4,'tile_1'=4] {'mem'}, dimensions={0} | all-to-all | bytes 3366912 | tf_op jit(solution)/shard_map/all_to_all | solution.py:50
  394.8 10.5 %all_to_all.44 = bf16[822,16,4]{0,2,1:T(4,128)(2,1)S(1)} all-to-all(bf16[822,16,4]{0,2,1:T(4,128)(2,1)S(1)} %multiply_convert_fusion.4), channel_id=1, replica_groups=mesh['mem'=8,'tile_0'=4,'tile_1'=4] {'tile_0','tile_1'}, dimensions={1} | all-to-all | bytes 210432 | tf_op jit(solution)/shard_map/all_to_all | solution.py:167
  405.5 17.0 %all_to_all.45 = bf16[8,822,16,4]{1,3,2,0:T(4,128)(2,1)S(1)} all-to-all(bf16[8,822,16,4]{1,3,2,0:T(4,128)(2,1)S(1)} %broadcast_in_dim.148), channel_id=1, replica_groups=mesh['mem'=8,'tile_0'=4,'tile_1'=4] {'mem'}, dimensions={0} | all-to-all | bytes 1683456 | tf_op jit(solution)/shard_map/all_to_all | solution.py:56
  424.2 5.0 %fusion.218 = f32[128,6,231]{2,1,0:T(8,128)S(1)} fusion(bf16[6,137,128]{1,0,2:T(8,128)(2,1)S(1)} %copy.185, bf16[128,231,137]{1,2,0:T(8,128)(2,1)} %copy.126), kind=kOutput, calls=%fused_computation.415 | convolution fusion | flops 48609792 | bytes 9021696 | tf_op jit(solution)/shard_map/ocl,plo->poc/dot_general | solution.py:174
  432.0 9.2 %all-reduce.1 = (f32[]{:T(128)}, f32[]{:T(128)}) all-reduce(f32[]{:T(128)} %get-tuple-element.434, f32[]{:T(128)} %get-tuple-element.384), channel_id=1, replica_groups=mesh['mem'=8,'tile_0'=4,'tile_1'=4] {'tile_0'}, use_global_device_ids=true, to_apply=%region_15.16 | all-reduce | flops 2 | bytes 16 | tf_op jit(solution)/shard_map/psum | solution.py:74
  441.3 9.6 %all-reduce = (f32[]{:T(128)}, f32[]{:T(128)}) all-reduce(f32[]{:T(128)} %get-tuple-element.382, f32[]{:T(128)} %get-tuple-element.383), channel_id=1, replica_groups=mesh['mem'=8,'tile_0'=4,'tile_1'=4] {'tile_1'}, use_global_device_ids=true, to_apply=%region_16.17 | all-reduce | flops 2 | bytes 16 | tf_op jit(solution)/shard_map/psum | solution.py:74
  (232 shorter events, 70.4 us)
Async XLA Ops:
  0.6 13.2 %copy-start.13 = (s32[3,128,231]{1,2,0:T(8,128)S(1)}, s32[3,128,231]{1,2,0:T(8,128)}, u32[]{:S(2)}) copy-start(s32[3,128,231]{1,2,0:T(8,128)} %param.14) | copy-start | bytes 1064452
  14.1 6.4 %copy-start.21 = (s32[128]{0:T(128)S(1)}, s32[128]{0:T(128)}, u32[]{:S(2)}) copy-start(s32[128]{0:T(128)} %param.17) | copy-start | bytes 1540
  14.1 6.4 %copy-start.22 = (s32[128]{0:T(128)S(1)}, s32[128]{0:T(128)}, u32[]{:S(2)}) copy-start(s32[128]{0:T(128)} %param.16) | copy-start | bytes 1540
  20.6 221.0 %copy-start.19 = (s32[128]{0:T(128)}, s32[128]{0:T(128)S(1)}, u32[]{:S(2)}) copy-start(s32[128]{0:T(128)S(1)} %multiply_add_fusion) | copy-start | bytes 1540
  22.5 52.2 %copy-start.14 = (bf16[2,137,512]{2,0,1:T(2,128)(2,1)S(1)}, bf16[2,137,512]{2,0,1:T(2,128)(2,1)}, u32[]{:S(2)}) copy-start(bf16[2,137,512]{2,0,1:T(2,128)(2,1)} %param.11) | copy-start | bytes 841732
  32.7 51.4 %all-to-all-start = ((bf16[16,411,32]{1,2,0:T(8,128)(2,1)}), bf16[16,411,32]{1,2,0:T(8,128)(2,1)S(1)}, u32[]{:S(2)}, u32[]{:S(2)}) async-start(bf16[16,411,32]{1,2,0:T(8,128)(2,1)} %constant_dynamic-update-slice_fusion), calls=%async_computation | async-start | bytes 1048576 | tf_op jit(solution)/shard_map/all_to_all | solution.py:139
  74.9 65.1 %copy-start.15 = (pred[16,8,4]{2,1,0:T(8,128)(4,1)}, pred[16,8,4]{2,1,0:T(8,128)(4,1)S(1)}, u32[]{:S(2)}) copy-start(pred[16,8,4]{2,1,0:T(8,128)(4,1)S(1)} %broadcast_in_dim.137) | copy-start | bytes 1540
  84.1 53.9 %copy-start.17 = (s32[1024]{0:T(1024)}, s32[1024]{0:T(1024)S(1)}, u32[]{:S(2)}) copy-start(s32[1024]{0:T(1024)S(1)} %pad_clamp_fusion) | copy-start | bytes 12292
  84.1 3.7 copy-start.8
  87.9 0.7 copy-start.2
  89.8 8.6 %collective-permute-start = (f32[3,137,192]{2,1,0:T(8,128)}, f32[3,137,192]{2,1,0:T(8,128)}, u32[]{:S(2)}, u32[]{:S(2)}) collective-permute-start(f32[3,137,192]{2,1,0:T(8,128)} %get-tuple-element.539), channel_id=1, source_target_pairs={{1,0},{2,1},{3,2},{4,3},{5,4},{6,5},{7,6},{8,7},{9,8},{10,9},{11,1... | collective-permute-start | bytes 946952 | tf_op jit(solution)/shard_map/while/body/eval_jaxpr/ppermute | solution.py:24
  91.9 11.7 %collective-permute-start.1 = (f32[3,137,192]{2,1,0:T(8,128)S(1)}, f32[3,137,192]{2,1,0:T(8,128)}, u32[]{:S(2)}, u32[]{:S(2)}) collective-permute-start(f32[3,137,192]{2,1,0:T(8,128)S(1)} %get-tuple-element.540), channel_id=1, source_target_pairs={{0,1},{1,2},{2,3},{3,4},{4,5},{5,6},{6,7},{7,8},{8,9},{9,10},{10,1... | collective-permute-start | bytes 946952 | tf_op jit(solution)/shard_map/while/body/eval_jaxpr/ppermute | solution.py:21
  112.2 1.1 copy-start.3
  113.3 0.7 copy-start.2
  115.2 8.6 %collective-permute-start = (f32[3,137,192]{2,1,0:T(8,128)}, f32[3,137,192]{2,1,0:T(8,128)}, u32[]{:S(2)}, u32[]{:S(2)}) collective-permute-start(f32[3,137,192]{2,1,0:T(8,128)} %get-tuple-element.539), channel_id=1, source_target_pairs={{1,0},{2,1},{3,2},{4,3},{5,4},{6,5},{7,6},{8,7},{9,8},{10,9},{11,1... | collective-permute-start | bytes 946952 | tf_op jit(solution)/shard_map/while/body/eval_jaxpr/ppermute | solution.py:24
  115.4 11.7 %collective-permute-start.1 = (f32[3,137,192]{2,1,0:T(8,128)S(1)}, f32[3,137,192]{2,1,0:T(8,128)}, u32[]{:S(2)}, u32[]{:S(2)}) collective-permute-start(f32[3,137,192]{2,1,0:T(8,128)S(1)} %get-tuple-element.540), channel_id=1, source_target_pairs={{0,1},{1,2},{2,3},{3,4},{4,5},{5,6},{6,7},{7,8},{8,9},{9,10},{10,1... | collective-permute-start | bytes 946952 | tf_op jit(solution)/shard_map/while/body/eval_jaxpr/ppermute | solution.py:21
  135.8 1.1 copy-start.3
  136.8 0.7 copy-start.4
  185.2 7.4 %copy-start.11 = (s32[3,128,231]{1,2,0:T(8,128)S(1)}, s32[3,128,231]{1,2,0:T(8,128)}, u32[]{:S(2)}) copy-start(s32[3,128,231]{1,2,0:T(8,128)} %param.15) | copy-start | bytes 1064452
  213.9 20.7 %copy-start.6 = (f32[3,128,231]{1,2,0:T(8,128)}, f32[3,128,231]{1,2,0:T(8,128)S(1)}, u32[]{:S(2)}) copy-start(f32[3,128,231]{1,2,0:T(8,128)S(1)} %get-tuple-element.389) | copy-start | bytes 1064452
  234.4 6.8 %copy-start.9 = (f32[3,128,231]{1,0,2:T(4,128)}, f32[3,128,231]{1,0,2:T(4,128)S(1)}, u32[]{:S(2)}) copy-start(f32[3,128,231]{1,0,2:T(4,128)S(1)} %fusion.190) | copy-start | bytes 1064452
  256.6 16.1 %all-to-all-start.4 = ((bf16[16,822,32]{1,2,0:T(8,128)(2,1)}), bf16[16,822,32]{1,2,0:T(8,128)(2,1)S(1)}, u32[]{:S(2)}, u32[]{:S(2)}) async-start(bf16[16,822,32]{1,2,0:T(8,128)(2,1)} %constant_dynamic-update-slice_fusion.16), calls=%async_computation.4 | async-start | bytes 1835008 | tf_op jit(solution)/shard_map/all_to_all | solution.py:139
  275.8 3.9 copy-start.5
  283.2 13.4 %collective-permute-start.2 = (f32[6,137,192]{2,1,0:T(8,128)}, f32[6,137,192]{2,1,0:T(8,128)}, u32[]{:S(2)}, u32[]{:S(2)}) collective-permute-start(f32[6,137,192]{2,1,0:T(8,128)} %get-tuple-element.558), channel_id=1, source_target_pairs={{1,0},{2,1},{3,2},{4,3},{5,4},{6,5},{7,6},{8,7},{9,8},{10,9},{11,1... | collective-permute-start | bytes 1893896 | tf_op jit(solution)/shard_map/while/body/eval_jaxpr/ppermute | solution.py:24
  284.4 16.5 %collective-permute-start.3 = (f32[6,137,192]{2,1,0:T(8,128)S(1)}, f32[6,137,192]{2,1,0:T(8,128)}, u32[]{:S(2)}, u32[]{:S(2)}) collective-permute-start(f32[6,137,192]{2,1,0:T(8,128)S(1)} %get-tuple-element.559), channel_id=1, source_target_pairs={{0,1},{1,2},{2,3},{3,4},{4,5},{5,6},{6,7},{7,8},{8,9},{9,10},{10,1... | collective-permute-start | bytes 1893896 | tf_op jit(solution)/shard_map/while/body/eval_jaxpr/ppermute | solution.py:21
  314.5 2.4 copy-start
  319.0 1.2 copy-start.1
  323.5 13.4 %collective-permute-start.2 = (f32[6,137,192]{2,1,0:T(8,128)}, f32[6,137,192]{2,1,0:T(8,128)}, u32[]{:S(2)}, u32[]{:S(2)}) collective-permute-start(f32[6,137,192]{2,1,0:T(8,128)} %get-tuple-element.558), channel_id=1, source_target_pairs={{1,0},{2,1},{3,2},{4,3},{5,4},{6,5},{7,6},{8,7},{9,8},{10,9},{11,1... | collective-permute-start | bytes 1893896 | tf_op jit(solution)/shard_map/while/body/eval_jaxpr/ppermute | solution.py:24
  323.7 16.5 %collective-permute-start.3 = (f32[6,137,192]{2,1,0:T(8,128)S(1)}, f32[6,137,192]{2,1,0:T(8,128)}, u32[]{:S(2)}, u32[]{:S(2)}) collective-permute-start(f32[6,137,192]{2,1,0:T(8,128)S(1)} %get-tuple-element.559), channel_id=1, source_target_pairs={{0,1},{1,2},{2,3},{3,4},{4,5},{5,6},{6,7},{7,8},{8,9},{9,10},{10,1... | collective-permute-start | bytes 1893896 | tf_op jit(solution)/shard_map/while/body/eval_jaxpr/ppermute | solution.py:21
  353.8 2.4 copy-start
  358.3 1.2 copy-start.1
  361.4 0.8 copy-start.18
  364.9 1.9 copy-start.16
  422.5 0.8 copy-start.20
  429.2 1.0 copy-start.7
  429.2 1.1 copy-start.10
  429.2 1.2 copy-start.12
